TPU v7x, 128 devices: a whole 4x4x4 slice. The times are simulated.
128 devices in a mesh: visit: 32 (over x, y, z_lo), tx: 2 (over core), ty: 2 (over z_hi).
Axes of the slice: x: 4, y: 4, z: 4 (z_hi: 2, z_lo: 2; z = z_hi * 2 + z_lo), core: 2. Of those that a mesh axis runs over, the one named last changes fastest.
Arguments:
- images: bfloat16 [32, 16, 128, 768], P('visit', None, 'ty', 'tx'), may hold values from -8 to 8
- partners: int32 [32, 16, 2], replicated, may hold values from 0 to 31, all different within a row; in each aligned block of 16 rows (0 to 15, 16 to 31, ..., all dimensions but the last counted through in order) at most 2 rows name the same one
- coverage: int32 [32, 16, 2, 16, 96], P('visit', None, None, 'ty', 'tx'), may hold values from 0 to 1, as said below
- x_filters: bfloat16 [40, 21], replicated, may hold values from -0.359375 to 0.359375
- row_filters: bfloat16 [40, 21], replicated, may hold values from -0.359375 to 0.359375
Outputs:
- coefficients: float32 [32, 16, 2, 40], P('visit', ('tx', 'ty'))
Inputs may be any that keep to these rules, and one draw needn't show every extreme that they name: In the 16 rows of one visit no visit is named more than 2 times, and in some visit's rows one visit is named exactly 2 times; the two partners of a tile differ. `coverage`: each mask is 1 on one rectangle of blocks that holds the tile's last block row and last block column, and 0 elsewhere.
All inputs are finite; a program needn't handle non-finite values.
Results may differ from a plain program's by a relative error of at most 0.00065.
Values may be sent and summed in bfloat16 or wider, within the bound.
A program may use at most 64 MiB of HBM per device.

v0:
```python
import functools

import jax
import jax.numpy as jnp
from jax import lax
from jax.experimental import pallas as pl
from jax.experimental.pallas import tpu as pltpu
from jax.sharding import PartitionSpec as P

CAP = 2
RIDGE_TERM = 0.002
NT = (((1,), (1,)), ((), ()))
VMEM = pltpu.VMEM
ANY = pl.ANY


def outgoing_tiles(requests, sender_visit, tile_count):
    is_sender = (requests == sender_visit).astype(jnp.int32)
    before = jnp.cumsum(is_sender, axis=1) - is_sender
    tile_ids = jnp.arange(2 * tile_count, dtype=jnp.int32)[None, :] // 2
    picked = [
        jnp.sum(jnp.where((is_sender == 1) & (before == slot), tile_ids, 0), axis=1)
        for slot in range(CAP)
    ]
    return jnp.stack(picked, axis=1).reshape(-1)


def arrival_slots(sources):
    count = sources.shape[0]
    same_source = sources[:, None] == sources[None, :]
    earlier = jnp.arange(count)[None, :] < jnp.arange(count)[:, None]
    return sources * CAP + jnp.sum((same_source & earlier).astype(jnp.int32), axis=1)


def send_pack_kernel(index_ref, tiles_ref, out_ref, sems):
    slots = out_ref.shape[0]

    def copy(slot):
        return pltpu.make_async_copy(
            tiles_ref.at[index_ref[slot]], out_ref.at[slot], sems.at[slot]
        )

    for slot in range(slots):
        copy(slot).start()
    for slot in range(slots):
        copy(slot).wait()


def send_pack(indices, tiles):
    slots = indices.shape[0]
    return pl.pallas_call(
        send_pack_kernel,
        out_shape=jax.ShapeDtypeStruct((slots,) + tiles.shape[1:], tiles.dtype),
        grid_spec=pltpu.PrefetchScalarGridSpec(
            num_scalar_prefetch=1,
            grid=(1,),
            in_specs=[pl.BlockSpec(tiles.shape, lambda i, s: (0, 0, 0))],
            out_specs=pl.BlockSpec(memory_space=ANY),
            scratch_shapes=[pltpu.SemaphoreType.DMA((slots,))],
        ),
    )(indices, tiles)


def group_pack_kernel(index_ref, arrived_ref, tiles_ref, out_ref, sems):
    owners, per_owner = out_ref.shape[0], out_ref.shape[1]
    science = tiles_ref.shape[0] // owners
    systems = per_owner - science
    copies = []
    for owner in range(owners):
        for place in range(systems):
            copies.append((arrived_ref.at[index_ref[owner * systems + place]], owner, place))
        for place in range(science):
            copies.append((tiles_ref.at[owner * science + place], owner, systems + place))
    started = []
    for number, (source, owner, place) in enumerate(copies):
        copy = pltpu.make_async_copy(source, out_ref.at[owner, place], sems.at[number])
        copy.start()
        started.append(copy)
    for copy in started:
        copy.wait()


def group_pack(indices, arrived, tiles, owners):
    tile_count = tiles.shape[0]
    per_owner = 3 * tile_count // owners
    shape = (owners, per_owner) + tiles.shape[1:]
    return pl.pallas_call(
        group_pack_kernel,
        out_shape=jax.ShapeDtypeStruct(shape, tiles.dtype),
        grid_spec=pltpu.PrefetchScalarGridSpec(
            num_scalar_prefetch=1,
            grid=(1,),
            in_specs=[pl.BlockSpec(memory_space=ANY), pl.BlockSpec(memory_space=ANY)],
            out_specs=pl.BlockSpec(shape, lambda i, s: (0, 0, 0, 0)),
            scratch_shapes=[pltpu.SemaphoreType.DMA((3 * tile_count,))],
        ),
    )(indices, arrived, tiles)


def tables_kernel(half_width, x_ref, y_ref, xtab_ref, ytab_ref):
    taps = x_ref.shape[1]
    step = pl.program_id(0)
    height = 128

    def toeplitz(ref, kernel, offsets):
        total = jnp.zeros(offsets.shape, jnp.float32)
        for tap in range(taps):
            total = jnp.where(offsets == tap, ref[kernel, tap], total)
        return total.astype(jnp.bfloat16)

    r = lax.broadcasted_iota(jnp.int32, (height, 128), 0)
    l = lax.broadcasted_iota(jnp.int32, (height, 128), 1)
    for place in range(2):
        kernel = 2 * step + place
        rows = slice(place * 128, place * 128 + 128)
        xtab_ref[0, rows] = toeplitz(x_ref, kernel, l - r)
        xtab_ref[1, rows] = toeplitz(x_ref, kernel, l + 128 - r)
        ytab_ref[0, place, rows] = toeplitz(y_ref, kernel, r - l + half_width)
        ytab_ref[0, 1 - place, rows] = jnp.zeros((128, 128), jnp.bfloat16)


def filter_tables(x_filters, row_filters, half_width):
    kernel_total, taps = x_filters.shape
    pairs = kernel_total // 2
    smem = pl.BlockSpec(memory_space=pltpu.SMEM)
    return pl.pallas_call(
        functools.partial(tables_kernel, half_width),
        out_shape=(
            jax.ShapeDtypeStruct((2, kernel_total * 128, 128), jnp.bfloat16),
            jax.ShapeDtypeStruct((pairs, 2, 256, 128), jnp.bfloat16),
        ),
        grid=(pairs,),
        in_specs=[smem, smem],
        out_specs=(
            pl.BlockSpec((2, 256, 128), lambda i: (0, i, 0)),
            pl.BlockSpec((1, 2, 256, 128), lambda i: (i, 0, 0, 0)),
        ),
        cost_estimate=pl.CostEstimate(flops=pairs * 21 * 400000, bytes_accessed=5 * 1024 * 1024, transcendentals=0),
    )(x_filters.astype(jnp.float32), row_filters.astype(jnp.float32))


def lane_tiles(ref, row_count):
    tiles = []
    for across in range(2):
        for tile in range(ref.shape[3] // 128):
            lanes = slice(tile * 128, tile * 128 + 128)
            tiles.append(jnp.concatenate([ref[2 * across, 0, :, lanes], ref[2 * across + 1, 0, :, lanes]], axis=0))
    return tiles


def normals_kernel(
    half_width, chunk, bounds_ref, template_ref, science_ref, xtab_ref, ytab_ref, out_ref,
    window, science, smooth, stack, mask, first, second, third,
):
    system = pl.program_id(0)
    row_start, col_start = bounds_ref[2 * system], bounds_ref[2 * system + 1]
    rows = 128
    pairs = ytab_ref.shape[0]
    kernel_total = 2 * pairs
    span = 2 * rows
    groups = span // 16
    tiles = lane_tiles(template_ref, rows)
    count = len(tiles)
    lane = lax.broadcasted_iota(jnp.int32, (rows, 128), 1)
    rolled = [pltpu.roll(tile.astype(jnp.float32), half_width, axis=1) for tile in tiles]
    zero = jnp.zeros((rows, 128), jnp.float32)
    for place in range(count + 1):
        before = rolled[place - 1] if place > 0 else zero
        here = rolled[place] if place < count else zero
        window[place] = jnp.where(lane < half_width, before, here).astype(jnp.bfloat16)
    for place, tile in enumerate(lane_tiles(science_ref, rows)):
        science[place] = tile
    first[...] = jnp.zeros_like(first)
    second[...] = jnp.zeros_like(second)
    third[...] = jnp.zeros_like(third)
    low, high, tall = 256, 512, 16 * (kernel_total + 1)

    def put(start, values):
        for group in range(groups):
            stack[group, pl.ds(start, 16), :] = values[group * 16 : group * 16 + 16]

    def part_body(part, carry):
        c = lax.broadcasted_iota(jnp.int32, (span, rows), 0) + part * span
        a = lax.broadcasted_iota(jnp.int32, (span, rows), 1)
        mask[...] = ((c >= col_start) & (a >= row_start)).astype(jnp.bfloat16)
        ones = (
            lax.broadcasted_iota(jnp.int32, (span, span), 0)
            == lax.broadcasted_iota(jnp.int32, (span, span), 1)
        ).astype(jnp.bfloat16)
        own = jnp.concatenate([science[2 * part], science[2 * part + 1]], axis=1)
        own = lax.dot_general(ones, own, NT, preferred_element_type=jnp.float32)
        put(kernel_total * 16, own.astype(jnp.bfloat16) * mask[...])

        left, middle, right = window[2 * part], window[2 * part + 1], window[2 * part + 2]
        data = jnp.concatenate(
            [jnp.concatenate([left, middle], axis=1), jnp.concatenate([middle, right], axis=1)], axis=0
        )

        def smooth_chunk(number):
            height = chunk * span
            base = number * height
            lhs = jnp.concatenate(
                [xtab_ref[0, pl.ds(base, height), :], xtab_ref[1, pl.ds(base, height), :]], axis=1
            )
            out = lax.dot_general(lhs, data, NT, preferred_element_type=jnp.float32).astype(jnp.bfloat16)
            slot = number % 2
            smooth[slot, 0] = out[:, :rows]
            smooth[slot, 1] = out[:, rows:]

        def basis_chunk(number):
            slot = number % 2
            for place in range(chunk):
                pair = number * chunk + place
                k1, k2 = slice(place * span, place * span + rows), slice(place * span + rows, place * span + span)
                lhs = jnp.concatenate(
                    [
                        jnp.concatenate([smooth[slot, 0, k1], smooth[slot, 0, k2]], axis=1),
                        jnp.concatenate([smooth[slot, 1, k1], smooth[slot, 1, k2]], axis=1),
                    ],
                    axis=0,
                )
                table = jnp.concatenate([ytab_ref[pair, 0], ytab_ref[pair, 1]], axis=1)
                basis = jnp.dot(lhs, table, preferred_element_type=jnp.float32).astype(jnp.bfloat16)
                base = pair * 32 if isinstance(pair, int) else pl.multiple_of(pair * 32, 32)
                put(base, basis[:, :rows] * mask[...])
                put(base + 16, basis[:, rows:] * mask[...])

        steps = pairs // chunk
        smooth_chunk(0)
        for number in range(steps):
            if number + 1 < steps:
                smooth_chunk(number + 1)
            basis_chunk(number)

        def operand(start, stop):
            return jnp.concatenate([stack[group, start:stop, :] for group in range(groups)], axis=1)

        def gram(lhs, rhs):
            return lax.dot_general(lhs, rhs, NT, preferred_element_type=jnp.float32)

        x0, x1, x2 = operand(0, low), operand(low, high), operand(high, tall)
        first[:low] += gram(x0, x0)
        first[low:] += gram(x2, x0)
        second[:low] += gram(x0, x1)
        second[low:high] += gram(x1, x1)
        second[high:] += gram(x2, x1)
        third[...] += gram(x2, x2)
        return carry

    lax.fori_loop(col_start // span, count * 128 // span, part_body, 0)

    def fold(ref):
        height, width = ref.shape
        r = lax.broadcasted_iota(jnp.int32, (height, width), 0)
        l = lax.broadcasted_iota(jnp.int32, (height, width), 1)
        kept = jnp.where((r % 16) == (l % 16), ref[...], 0.0)
        summed = jnp.sum(kept.reshape(height // 16, 16, width), axis=1)
        s = lax.broadcasted_iota(jnp.int32, (width, 128), 0)
        t = lax.broadcasted_iota(jnp.int32, (width, 128), 1)
        return jnp.dot(
            summed, ((s // 16) == t).astype(jnp.float32),
            preferred_element_type=jnp.float32, precision=lax.Precision.HIGHEST,
        )

    out_ref[0, 0:25] = fold(first)
    out_ref[0, 32:73] = fold(second)
    out_ref[0, 80:89] = fold(third)


CHUNK = 4


def normals(bounds, gathered, xtab, ytab, half_width):
    owners, per_owner, half_rows, half_cols = gathered.shape
    systems = 2 * per_owner // 3
    rows, cols = 2 * half_rows, 2 * half_cols
    span = 2 * rows
    quarter = (owners, 1, half_rows, half_cols)
    kernel_total = 2 * ytab.shape[0]
    tall = 16 * (kernel_total + 1)
    return pl.pallas_call(
        functools.partial(normals_kernel, half_width, CHUNK),
        out_shape=jax.ShapeDtypeStruct((systems, 96, 128), jnp.float32),
        grid_spec=pltpu.PrefetchScalarGridSpec(
            num_scalar_prefetch=1,
            grid=(systems,),
            in_specs=[
                pl.BlockSpec(quarter, lambda i, s: (0, i, 0, 0)),
                pl.BlockSpec(quarter, lambda i, s: (0, systems + i // 2, 0, 0)),
                pl.BlockSpec(xtab.shape, lambda i, s: (0, 0, 0)),
                pl.BlockSpec(ytab.shape, lambda i, s: (0, 0, 0, 0)),
            ],
            out_specs=pl.BlockSpec((1, 96, 128), lambda i, s: (i, 0, 0)),
            scratch_shapes=[
                VMEM((cols // 128 + 1, rows, 128), jnp.bfloat16),
                VMEM((cols // 128, rows, 128), jnp.bfloat16),
                VMEM((2, 2, CHUNK * span, rows), jnp.bfloat16),
                VMEM((span // 16, tall, rows), jnp.bfloat16),
                VMEM((span, rows), jnp.bfloat16),
                VMEM((256 + tall - 512, 256), jnp.float32),
                VMEM((tall, 256), jnp.float32),
                VMEM((tall - 512, tall - 512), jnp.float32),
            ],
        ),
        compiler_params=pltpu.CompilerParams(vmem_limit_bytes=56 * 1024 * 1024),
    )(bounds, gathered, gathered, xtab, ytab)


def solve_kernel(kernel_total, pixel_values, blocks_ref, out_ref):
    systems = blocks_ref.shape[0]
    r = lax.broadcasted_iota(jnp.int32, (128, 128), 0)
    l = lax.broadcasted_iota(jnp.int32, (128, 128), 1)
    matrices = []
    for system in range(systems):
        blocks = blocks_ref[system]
        first, second, third = blocks[0:32], blocks[32:80], blocks[80:96]
        zero = jnp.zeros((16, 128), jnp.float32)
        left = jnp.concatenate([first[:16], zero, first[16:32]] + [zero] * 5, axis=0)
        middle = jnp.concatenate([pltpu.roll(second, 16, axis=1)] + [zero] * 5, axis=0)
        right = jnp.concatenate([zero, zero, pltpu.roll(third, 32, axis=1)] + [zero] * 5, axis=0)
        left = jnp.where((l < 16) & ((r < 16) | ((r >= 32) & (r <= kernel_total))), left, 0.0)
        middle = jnp.where((l >= 16) & (l < 32) & (r <= kernel_total), middle, 0.0)
        right = jnp.where((l >= 32) & (l <= kernel_total) & (r >= 32) & (r <= kernel_total), right, 0.0)
        known = left + middle + right
        other = jnp.transpose(known)
        absent = ((r >= 16) & (r < 32) & (l < 16)) | ((l >= 32) & (r < 32))
        whole = jnp.where(absent, other, known) / pixel_values
        whole = whole + jnp.where((r == l) & (r < kernel_total), RIDGE_TERM, 0.0)
        matrices.append(whole[:kernel_total])
    work = jnp.stack(matrices, axis=0)
    row_ids = lax.broadcasted_iota(jnp.int32, (1, kernel_total, 1), 1)
    for pivot in range(kernel_total):
        row = work[:, pivot : pivot + 1, :]
        row = row / row[:, :, pivot : pivot + 1]
        column = work[:, :, pivot : pivot + 1]
        work = jnp.where(row_ids == pivot, row, work - column * row)
    lanes = lax.broadcasted_iota(jnp.int32, work.shape, 2)
    out_ref[...] = jnp.sum(jnp.where(lanes == kernel_total, work, 0.0), axis=2)


def solve(blocks, kernel_total, pixel_values):
    return pl.pallas_call(
        functools.partial(solve_kernel, kernel_total, float(pixel_values)),
        out_shape=jax.ShapeDtypeStruct((blocks.shape[0], kernel_total), jnp.float32),
    )(blocks)


def body(images, partners, coverage, x_filters, row_filters):
    visit = lax.axis_index("visit")
    own_tiles = images[0]
    tile_count, row_count, col_count = own_tiles.shape
    half_width = (x_filters.shape[1] - 1) // 2
    kernel_total = x_filters.shape[0]
    visit_count = partners.shape[0]
    owners = lax.axis_size("tx") * lax.axis_size("ty")
    requests = partners.reshape(visit_count, 2 * tile_count)
    own_requests = lax.dynamic_index_in_dim(requests, visit, 0, keepdims=False)
    sent = send_pack(outgoing_tiles(requests, visit, tile_count), own_tiles)
    arrived = lax.all_to_all(
        sent.reshape((visit_count, CAP) + own_tiles.shape[1:]), "visit", split_axis=0, concat_axis=0, tiled=True
    )
    arrived = arrived.reshape((visit_count * CAP,) + own_tiles.shape[1:])
    grouped = group_pack(arrival_slots(own_requests), arrived, own_tiles, owners)
    gathered = lax.all_to_all(grouped, ("tx", "ty"), split_axis=0, concat_axis=0, tiled=True)

    blocks = coverage[0]
    block_size = row_count // blocks.shape[2]
    row_blocks = jnp.max(blocks, axis=3).sum(axis=2)
    col_blocks = jnp.max(blocks, axis=2).sum(axis=2)
    counts = jnp.stack([row_blocks, col_blocks], axis=-1).astype(jnp.float32)
    counts = lax.all_to_all(
        counts.reshape(owners, 2 * tile_count // owners, 2), ("tx", "ty"), split_axis=0, concat_axis=0, tiled=True
    )
    row_start = 2 * row_count - block_size * (counts[2, :, 0] + counts[3, :, 0])
    col_start = 2 * col_count - block_size * (counts[1, :, 1] + counts[3, :, 1])
    bounds = jnp.stack([row_start, col_start], axis=-1).astype(jnp.int32).reshape(-1)

    xtab, ytab = filter_tables(x_filters, row_filters, half_width)
    sums = normals(bounds, gathered, xtab, ytab, half_width)
    pixel_values = row_count * col_count * owners
    coefficients = solve(sums, kernel_total, pixel_values)
    return coefficients.reshape(1, tile_count // owners, 2, kernel_total)


def solution(mesh):
    return jax.shard_map(
        body,
        mesh=mesh,
        in_specs=(P("visit", None, "ty", "tx"), P(), P("visit", None, None, "ty", "tx"), P(), P()),
        out_specs=P("visit", ("tx", "ty"), None, None),
        check_vma=False,
    )
```

profile of v0, /device:TPU:35, one launch (start us, length us, event | category | flops | bytes accessed | tf_op | source)
XLA Modules:
  0.0 184.2 jit_solution(13044104269350305394)
XLA Ops:
  0.0 0.8 copy.56
  0.8 0.2 reduce_window_sum.13
  1.0 0.1 copy.58
  1.1 0.8 fusion
  1.9 0.1 copy.59
  2.0 0.6 reshape.133.index_ref
  2.6 4.0 %shard_map.55 = bf16[64,64,384]{2,1,0:T(8,128)(2,1)} custom-call(s32[64]{0:T(128)} %reshape.133.index_ref, bf16[16,64,384]{2,1,0:T(8,128)(2,1)} %bitcast.18), custom_call_target="tpu_custom_call" | custom-call | tf_op jit(solution)/shard_map/pallas_call | solution.py:51
  6.7 0.0 copy-start.2
  6.7 8.1 %all-to-all-start.1 = ((bf16[32,2,64,384]{3,2,1,0:T(8,128)(2,1)}), bf16[32,2,64,384]{3,2,1,0:T(8,128)(2,1)S(1)}, u32[]{:S(2)}, u32[]{:S(2)}) async-start(bf16[32,2,64,384]{3,2,1,0:T(8,128)(2,1)} %bitcast.17), calls=%async_computation.1 | async-start | bytes 6291456 | tf_op jit(solution)/shard_map/all_to_all | solution.py:359
  14.8 0.0 copy-done.2
  14.8 0.7 fusion.8
  15.5 0.3 reduce_sum.45
  15.8 0.3 reduce_sum.46
  16.2 0.1 stack.24
  16.3 0.1 stack.23
  16.3 0.6 copy.54
  17.0 0.2 convert_reduce_fusion
  17.1 35.7 %all-to-all-done.1 = bf16[32,2,64,384]{3,2,1,0:T(8,128)(2,1)S(1)} async-done(((bf16[32,2,64,384]{3,2,1,0:T(8,128)(2,1)}), bf16[32,2,64,384]{3,2,1,0:T(8,128)(2,1)S(1)}, u32[]{:S(2)}, u32[]{:S(2)}) %all-to-all-start.1) | async-done | bytes 3145760 | tf_op jit(solution)/shard_map/all_to_all | solution.py:359
  52.8 0.0 copy-start.1
  52.8 6.7 %all-to-all-start = ((f32[4,8,2]{1,2,0:T(2,128)}), f32[4,8,2]{1,2,0:T(2,128)S(1)}, u32[]{:S(2)}, u32[]{:S(2)}) async-start(f32[4,8,2]{1,2,0:T(2,128)} %copy.54), calls=%async_computation | async-start | bytes 8192 | tf_op jit(solution)/shard_map/all_to_all | solution.py:371
  59.5 0.5 multiply_add_fusion.1.index_ref
  59.9 0.0 copy-done.1
  60.0 4.1 %shard_map.56 = bf16[4,12,64,384]{3,2,1,0:T(8,128)(2,1)} custom-call(s32[32]{0:T(128)} %multiply_add_fusion.1.index_ref, bf16[64,64,384]{2,1,0:T(8,128)(2,1)} %bitcast.16, bf16[16,64,384]{2,1,0:T(8,128)(2,1)} %bitcast.19), custom_call_target="tpu_custom_call" | custom-call | tf_op jit(solution)/shard_map/pallas_call | solution.py:87
  64.1 0.0 copy-start.3
  64.1 0.0 copy-start.4
  64.1 0.0 all-to-all-done
  64.1 4.8 %all-to-all-start.2 = ((bf16[4,12,64,384]{3,2,1,0:T(8,128)(2,1)}), bf16[4,12,64,384]{3,2,1,0:T(8,128)(2,1)S(1)}, u32[]{:S(2)}, u32[]{:S(2)}) async-start(bf16[4,12,64,384]{3,2,1,0:T(8,128)(2,1)} %shard_map.56), calls=%async_computation.2 | async-start | bytes 4718592 | tf_op jit(solution)/shard_map/all_to_all | solution.py:364
  69.0 0.0 copy-done.3
  69.0 0.7 copy.60.x_ref
  69.6 0.0 copy-done.4
  69.6 0.7 copy.61.y_ref
  70.3 14.1 %shard_map.57 = (bf16[2,5120,128]{2,1,0:T(8,128)(2,1)}, bf16[20,2,256,128]{3,2,1,0:T(8,128)(2,1)}) custom-call(f32[40,21]{1,0:T(8,128)} %copy.60.x_ref, f32[40,21]{1,0:T(8,128)} %copy.61.y_ref), custom_call_target="tpu_custom_call" | custom-call | flops 168000000 | bytes 5242880 | tf_op jit(solution)/shard_map/pallas_call | solution.py:126
  84.4 0.1 copy.55
  84.5 0.6 convert_element_type.29.bounds_ref
  85.1 12.9 %all-to-all-done.2.template_ref.science_ref = bf16[4,12,64,384]{3,2,1,0:T(8,128)(2,1)S(1)} async-done(((bf16[4,12,64,384]{3,2,1,0:T(8,128)(2,1)}), bf16[4,12,64,384]{3,2,1,0:T(8,128)(2,1)S(1)}, u32[]{:S(2)}, u32[]{:S(2)}) %all-to-all-start.2) | async-done | bytes 2359328 | tf_op jit(solution)/shard_map/all_to_all | solution.py:364
  98.0 0.0 copy-start
  98.0 1.4 copy-done
  99.4 79.0 %shard_map.58.blocks_ref = f32[8,96,128]{2,1,0:T(8,128)} custom-call(s32[16]{0:T(128)} %convert_element_type.29.bounds_ref, bf16[4,12,64,384]{3,2,1,0:T(8,128)(2,1)} %copy-done, bf16[4,12,64,384]{3,2,1,0:T(8,128)(2,1)} %copy-done, bf16[2,5120,128]{2,1,0:T(8,128)(2,1)} %get-tuple-element.7.xtab_ref, bf16[20,2,256,128]{3,2,1,0:T(8,128)(2,1)} %get-tuple-element.8.ytab_ref), custom_call_target="tpu_custom_call" | custom-call | tf_op jit(solution)/shard_map/pallas_call | solution.py:281
  178.5 5.7 %shard_map.59 = f32[8,40]{1,0:T(8,128)} custom-call(f32[8,96,128]{2,1,0:T(8,128)} %shard_map.58.blocks_ref), custom_call_target="tpu_custom_call" | custom-call | tf_op jit(solution)/shard_map/pallas_call | solution.py:342
  (7 shorter events, 0.1 us)
Async XLA Ops:
  6.7 8.1 %copy-start.2 = (s32[1,16,2,8,48]{4,3,2,1,0:T(8,128)S(1)}, s32[1,16,2,8,48]{4,3,2,1,0:T(8,128)}, u32[]{:S(2)}) copy-start(s32[1,16,2,8,48]{4,3,2,1,0:T(8,128)} %param.7) | copy-start | bytes 147460
  6.7 46.1 %all-to-all-start.1 = ((bf16[32,2,64,384]{3,2,1,0:T(8,128)(2,1)}), bf16[32,2,64,384]{3,2,1,0:T(8,128)(2,1)S(1)}, u32[]{:S(2)}, u32[]{:S(2)}) async-start(bf16[32,2,64,384]{3,2,1,0:T(8,128)(2,1)} %bitcast.17), calls=%async_computation.1 | async-start | bytes 6291456 | tf_op jit(solution)/shard_map/all_to_all | solution.py:359
  52.8 7.1 %copy-start.1 = (bf16[32,2,64,384]{3,2,1,0:T(8,128)(2,1)}, bf16[32,2,64,384]{3,2,1,0:T(8,128)(2,1)S(1)}, u32[]{:S(2)}) copy-start(bf16[32,2,64,384]{3,2,1,0:T(8,128)(2,1)S(1)} %all-to-all-done.1) | copy-start | bytes 9437188
  52.8 11.3 %all-to-all-start = ((f32[4,8,2]{1,2,0:T(2,128)}), f32[4,8,2]{1,2,0:T(2,128)S(1)}, u32[]{:S(2)}, u32[]{:S(2)}) async-start(f32[4,8,2]{1,2,0:T(2,128)} %copy.54), calls=%async_computation | async-start | bytes 8192 | tf_op jit(solution)/shard_map/all_to_all | solution.py:371
  64.1 4.8 %copy-start.3 = (bf16[40,21]{0,1:T(8,128)(2,1)S(1)}, bf16[40,21]{0,1:T(8,128)(2,1)}, u32[]{:S(2)}) copy-start(bf16[40,21]{0,1:T(8,128)(2,1)} %param.8) | copy-start | bytes 5044
  64.1 5.5 %copy-start.4 = (bf16[40,21]{0,1:T(8,128)(2,1)S(1)}, bf16[40,21]{0,1:T(8,128)(2,1)}, u32[]{:S(2)}) copy-start(bf16[40,21]{0,1:T(8,128)(2,1)} %param.9) | copy-start | bytes 5044
  64.1 33.8 %all-to-all-start.2 = ((bf16[4,12,64,384]{3,2,1,0:T(8,128)(2,1)}), bf16[4,12,64,384]{3,2,1,0:T(8,128)(2,1)S(1)}, u32[]{:S(2)}, u32[]{:S(2)}) async-start(bf16[4,12,64,384]{3,2,1,0:T(8,128)(2,1)} %shard_map.56), calls=%async_computation.2 | async-start | bytes 4718592 | tf_op jit(solution)/shard_map/all_to_all | solution.py:364
  98.0 1.5 copy-start
where the time goes:
time: 186 us; the launch traced here: 184 us
  Pallas kernels  107 us (58%)
  waiting for transfers between devices  48.5 us (26%)
  starting transfers between devices  19.6 us (11%)
  local copies, waits for them, and re-layouts  5.86 us (3%)
  other arithmetic  3.1 us (2%)
    pallas_call x1, Pallas kernels, normals(): pl.pallas_call(functools.partial(normals_kernel, half_width, CHUNK), out_...  79 us
    all_to_all x1, waiting for transfers between devices, body(): lax.all_to_all(sent.reshape((visit_count, CAP) + own_tiles.shape[1:]), 'v...  35.7 us
    pallas_call x1, Pallas kernels, filter_tables(): pl.pallas_call(functools.partial(tables_kernel, half_width), out_shape=(j...  14.1 us
    all_to_all x1, waiting for transfers between devices, body(): lax.all_to_all(grouped, ('tx', 'ty'), split_axis=0, concat_axis=0, tiled=...  12.9 us
    all_to_all x1, starting transfers between devices, body(): lax.all_to_all(sent.reshape((visit_count, CAP) + own_tiles.shape[1:]), 'v...  8.1 us
    all_to_all x1, starting transfers between devices, body(): lax.all_to_all(counts.reshape(owners, 2 * tile_count // owners, 2), ('tx'...  6.65 us
    pallas_call x1, Pallas kernels, solve(): pl.pallas_call(functools.partial(solve_kernel, kernel_total, float(pixel_...  5.73 us
    all_to_all x1, starting transfers between devices, body(): lax.all_to_all(grouped, ('tx', 'ty'), split_axis=0, concat_axis=0, tiled=...  4.81 us
  transfers between devices with their start and end apart: 3, of which 2 were waited for; matrix products, arithmetic and copies ran while one was open for 3% of the time, Pallas kernels for 10%

commit v1 on v0

--- a/solution.py
+++ b/solution.py
@@ -32,111 +32,168 @@
     return sources * CAP + jnp.sum((same_source & earlier).astype(jnp.int32), axis=1)
 
 
-def send_pack_kernel(index_ref, tiles_ref, out_ref, sems):
-    slots = out_ref.shape[0]
-
-    def copy(slot):
-        return pltpu.make_async_copy(
-            tiles_ref.at[index_ref[slot]], out_ref.at[slot], sems.at[slot]
-        )
-
-    for slot in range(slots):
-        copy(slot).start()
-    for slot in range(slots):
-        copy(slot).wait()
-
-
-def send_pack(indices, tiles):
-    slots = indices.shape[0]
+MESH = pl.DeviceIdType.MESH
+GROUP = ((0, 1), (1, 1), (1, 0))
+
+
+def exchange_kernel(
+    send_ref, slot_ref, tiles, counts, out, counts_out, send_a, recv_a, send_b,
+    sent_a, got_a, sent_b, got_b, sent_c, got_c, sent_d, got_d, local,
+):
+    visits = lax.axis_size("visit")
+    visit, tx, ty = lax.axis_index("visit"), lax.axis_index("tx"), lax.axis_index("ty")
+    own = tx * 2 + ty
+    owners, systems = out.shape[0], slot_ref.shape[0] // out.shape[0]
+    share = tiles.shape[0] // owners
+
+    def pack(place, carry):
+        for slot in range(CAP):
+            send_a[place, slot] = tiles[send_ref[CAP * place + slot]]
+        return carry
+
+    lax.fori_loop(0, visits, pack, 0)
+
+    barrier = pltpu.get_barrier_semaphore()
+    for step in range(1, visits):
+        pl.semaphore_signal(barrier, inc=1, device_id=((visit + step) % visits, tx, ty), device_id_type=MESH)
+    for dx, dy in GROUP:
+        pl.semaphore_signal(barrier, inc=1, device_id=(visit, (tx + dx) % 2, (ty + dy) % 2), device_id_type=MESH)
+    pl.semaphore_wait(barrier, visits - 1 + len(GROUP))
+
+    copies_a = []
+    for step in range(1, visits):
+        target = (visit + step) % visits
+        copies_a.append(
+            pltpu.make_async_remote_copy(
+                send_a.at[target], recv_a.at[pl.ds(visit * CAP, CAP)], sent_a.at[step], got_a.at[step],
+                device_id=(target, tx, ty), device_id_type=MESH,
+            )
+        )
+    copies_b, copies_c = [], []
+    for number, (dx, dy) in enumerate(GROUP):
+        px, py = (tx + dx) % 2, (ty + dy) % 2
+        peer = px * 2 + py
+        place = dict(device_id=(visit, px, py), device_id_type=MESH)
+        copies_c.append(
+            pltpu.make_async_remote_copy(
+                tiles.at[pl.ds(share * peer, share)], out.at[own, pl.ds(systems, share)],
+                sent_c.at[number], got_c.at[number], **place,
+            )
+        )
+        copies_c.append(
+            pltpu.make_async_remote_copy(
+                counts.at[peer], counts_out.at[own], sent_d.at[number], got_d.at[number], **place,
+            )
+        )
+        copies_b.append(
+            pltpu.make_async_remote_copy(
+                send_b.at[peer], out.at[own, pl.ds(0, systems)], sent_b.at[number], got_b.at[number], **place,
+            )
+        )
+    keep = pltpu.make_async_copy(send_a.at[visit], recv_a.at[pl.ds(visit * CAP, CAP)], local.at[0])
+    science = pltpu.make_async_copy(
+        tiles.at[pl.ds(share * own, share)], out.at[own, pl.ds(systems, share)], local.at[1]
+    )
+    tally = pltpu.make_async_copy(counts.at[own], counts_out.at[own], local.at[2])
+    last = pltpu.make_async_copy(send_b.at[own], out.at[own, pl.ds(0, systems)], local.at[3])
+    for copy in copies_a:
+        copy.start()
+    keep.start()
+    for copy in copies_c:
+        copy.start()
+    science.start()
+    tally.start()
+    keep.wait()
+    for copy in copies_a:
+        copy.wait_recv()
+    for number, (dx, dy) in enumerate(GROUP):
+        peer = ((tx + dx) % 2) * 2 + (ty + dy) % 2
+        for place in range(systems):
+            send_b[peer, place] = recv_a[slot_ref[peer * systems + place]]
+        copies_b[number].start()
+    for place in range(systems):
+        send_b[own, place] = recv_a[slot_ref[own * systems + place]]
+    last.start()
+    for copy in copies_b:
+        copy.wait()
+    for copy in copies_c:
+        copy.wait()
+    for copy in copies_a:
+        copy.wait_send()
+    science.wait()
+    tally.wait()
+    last.wait()
+
+
+def exchange(send_index, slot_index, tiles, counts):
+    owners = counts.shape[0]
+    tile_count = tiles.shape[0]
+    tile = tiles.shape[1:]
+    slots = send_index.shape[0]
+    systems = 2 * tile_count // owners
+    smem, vmem = pl.BlockSpec(memory_space=pltpu.SMEM), pl.BlockSpec(memory_space=VMEM)
+    dma = pltpu.SemaphoreType.DMA
+    peers = len(GROUP)
     return pl.pallas_call(
-        send_pack_kernel,
-        out_shape=jax.ShapeDtypeStruct((slots,) + tiles.shape[1:], tiles.dtype),
-        grid_spec=pltpu.PrefetchScalarGridSpec(
-            num_scalar_prefetch=1,
-            grid=(1,),
-            in_specs=[pl.BlockSpec(tiles.shape, lambda i, s: (0, 0, 0))],
-            out_specs=pl.BlockSpec(memory_space=ANY),
-            scratch_shapes=[pltpu.SemaphoreType.DMA((slots,))],
+        exchange_kernel,
+        out_shape=(
+            jax.ShapeDtypeStruct((owners, 3 * tile_count // owners) + tile, tiles.dtype),
+            jax.ShapeDtypeStruct(counts.shape, counts.dtype),
         ),
-    )(indices, tiles)
-
-
-def group_pack_kernel(index_ref, arrived_ref, tiles_ref, out_ref, sems):
-    owners, per_owner = out_ref.shape[0], out_ref.shape[1]
-    science = tiles_ref.shape[0] // owners
-    systems = per_owner - science
-    copies = []
-    for owner in range(owners):
-        for place in range(systems):
-            copies.append((arrived_ref.at[index_ref[owner * systems + place]], owner, place))
-        for place in range(science):
-            copies.append((tiles_ref.at[owner * science + place], owner, systems + place))
-    started = []
-    for number, (source, owner, place) in enumerate(copies):
-        copy = pltpu.make_async_copy(source, out_ref.at[owner, place], sems.at[number])
-        copy.start()
-        started.append(copy)
-    for copy in started:
-        copy.wait()
-
-
-def group_pack(indices, arrived, tiles, owners):
-    tile_count = tiles.shape[0]
-    per_owner = 3 * tile_count // owners
-    shape = (owners, per_owner) + tiles.shape[1:]
-    return pl.pallas_call(
-        group_pack_kernel,
-        out_shape=jax.ShapeDtypeStruct(shape, tiles.dtype),
-        grid_spec=pltpu.PrefetchScalarGridSpec(
-            num_scalar_prefetch=1,
-            grid=(1,),
-            in_specs=[pl.BlockSpec(memory_space=ANY), pl.BlockSpec(memory_space=ANY)],
-            out_specs=pl.BlockSpec(shape, lambda i, s: (0, 0, 0, 0)),
-            scratch_shapes=[pltpu.SemaphoreType.DMA((3 * tile_count,))],
-        ),
-    )(indices, arrived, tiles)
+        in_specs=[smem, smem, vmem, vmem],
+        out_specs=(pl.BlockSpec(memory_space=ANY), vmem),
+        scratch_shapes=[
+            VMEM((slots // CAP, CAP) + tile, tiles.dtype),
+            VMEM((slots,) + tile, tiles.dtype),
+            VMEM((owners, systems) + tile, tiles.dtype),
+            dma((slots // CAP,)), dma((slots // CAP,)),
+            dma((peers,)), dma((peers,)), dma((peers,)), dma((peers,)), dma((peers,)), dma((peers,)),
+            dma((4,)),
+        ],
+        compiler_params=pltpu.CompilerParams(collective_id=0, has_side_effects=True),
+    )(send_index, slot_index, tiles, counts)
 
 
 def tables_kernel(half_width, x_ref, y_ref, xtab_ref, ytab_ref):
-    taps = x_ref.shape[1]
-    step = pl.program_id(0)
     height = 128
-
-    def toeplitz(ref, kernel, offsets):
-        total = jnp.zeros(offsets.shape, jnp.float32)
-        for tap in range(taps):
-            total = jnp.where(offsets == tap, ref[kernel, tap], total)
-        return total.astype(jnp.bfloat16)
-
     r = lax.broadcasted_iota(jnp.int32, (height, 128), 0)
     l = lax.broadcasted_iota(jnp.int32, (height, 128), 1)
-    for place in range(2):
-        kernel = 2 * step + place
-        rows = slice(place * 128, place * 128 + 128)
-        xtab_ref[0, rows] = toeplitz(x_ref, kernel, l - r)
-        xtab_ref[1, rows] = toeplitz(x_ref, kernel, l + 128 - r)
-        ytab_ref[0, place, rows] = toeplitz(y_ref, kernel, r - l + half_width)
-        ytab_ref[0, 1 - place, rows] = jnp.zeros((128, 128), jnp.bfloat16)
+    near = jnp.abs(r - l) <= half_width
+
+    def shifted(row):
+        return pltpu.roll(jnp.broadcast_to(row, (height, row.shape[1])), 0, axis=1, stride=1, stride_axis=0)
+
+    def body(pair, carry):
+        for place in range(2):
+            kernel = 2 * pair + place
+            rows = pl.ds(pl.multiple_of(kernel * height, height), height)
+            table = shifted(x_ref[pl.ds(kernel, 1), :]).astype(jnp.bfloat16)
+            xtab_ref[0, rows] = table[:, :128]
+            xtab_ref[1, rows] = table[:, 128:]
+            table = jnp.where(near, shifted(y_ref[pl.ds(kernel, 1), :]), 0.0).astype(jnp.bfloat16)
+            half = slice(place * height, place * height + height)
+            ytab_ref[pair, place, half] = table
+            ytab_ref[pair, 1 - place, half] = jnp.zeros((height, 128), jnp.bfloat16)
+        return carry
+
+    lax.fori_loop(0, ytab_ref.shape[0], body, 0)
 
 
 def filter_tables(x_filters, row_filters, half_width):
     kernel_total, taps = x_filters.shape
     pairs = kernel_total // 2
-    smem = pl.BlockSpec(memory_space=pltpu.SMEM)
+    x_rows = jnp.pad(x_filters.astype(jnp.float32), ((0, 0), (0, 256 - taps)))
+    y_rows = row_filters[:, ::-1].astype(jnp.float32)
+    y_rows = jnp.concatenate(
+        [y_rows[:, half_width:], jnp.zeros((kernel_total, 128 - taps), jnp.float32), y_rows[:, :half_width]], axis=1
+    )
     return pl.pallas_call(
         functools.partial(tables_kernel, half_width),
         out_shape=(
             jax.ShapeDtypeStruct((2, kernel_total * 128, 128), jnp.bfloat16),
             jax.ShapeDtypeStruct((pairs, 2, 256, 128), jnp.bfloat16),
         ),
-        grid=(pairs,),
-        in_specs=[smem, smem],
-        out_specs=(
-            pl.BlockSpec((2, 256, 128), lambda i: (0, i, 0)),
-            pl.BlockSpec((1, 2, 256, 128), lambda i: (i, 0, 0, 0)),
-        ),
-        cost_estimate=pl.CostEstimate(flops=pairs * 21 * 400000, bytes_accessed=5 * 1024 * 1024, transcendentals=0),
-    )(x_filters.astype(jnp.float32), row_filters.astype(jnp.float32))
+    )(x_rows, y_rows)
 
 
 def lane_tiles(ref, row_count):
@@ -355,21 +412,14 @@
     owners = lax.axis_size("tx") * lax.axis_size("ty")
     requests = partners.reshape(visit_count, 2 * tile_count)
     own_requests = lax.dynamic_index_in_dim(requests, visit, 0, keepdims=False)
-    sent = send_pack(outgoing_tiles(requests, visit, tile_count), own_tiles)
-    arrived = lax.all_to_all(
-        sent.reshape((visit_count, CAP) + own_tiles.shape[1:]), "visit", split_axis=0, concat_axis=0, tiled=True
-    )
-    arrived = arrived.reshape((visit_count * CAP,) + own_tiles.shape[1:])
-    grouped = group_pack(arrival_slots(own_requests), arrived, own_tiles, owners)
-    gathered = lax.all_to_all(grouped, ("tx", "ty"), split_axis=0, concat_axis=0, tiled=True)
-
     blocks = coverage[0]
     block_size = row_count // blocks.shape[2]
     row_blocks = jnp.max(blocks, axis=3).sum(axis=2)
     col_blocks = jnp.max(blocks, axis=2).sum(axis=2)
     counts = jnp.stack([row_blocks, col_blocks], axis=-1).astype(jnp.float32)
-    counts = lax.all_to_all(
-        counts.reshape(owners, 2 * tile_count // owners, 2), ("tx", "ty"), split_axis=0, concat_axis=0, tiled=True
+    counts = jnp.pad(counts.reshape(owners, 2 * tile_count // owners, 2), ((0, 0), (0, 0), (0, 126)))
+    gathered, counts = exchange(
+        outgoing_tiles(requests, visit, tile_count), arrival_slots(own_requests), own_tiles, counts
     )
     row_start = 2 * row_count - block_size * (counts[2, :, 0] + counts[3, :, 0])
     col_start = 2 * col_count - block_size * (counts[1, :, 1] + counts[3, :, 1])

time: 186 us -> 201 us (1.081)
  the two profiles are of different devices: /device:TPU:35 before, /device:TPU:125 now
where the time goes in v1:
time: 201 us; the launch traced here: 203 us
  Pallas kernels  192 us (96%)
  other arithmetic  6.29 us (3%)
  local copies, waits for them, and re-layouts  4.94 us (2%)
    pallas_call x1, Pallas kernels, exchange(): pl.pallas_call(exchange_kernel, out_shape=(jax.ShapeDtypeStruct((owners,...  108 us
    pallas_call x1, Pallas kernels, normals(): pl.pallas_call(functools.partial(normals_kernel, half_width, CHUNK), out_...  72.8 us
    pallas_call x1, Pallas kernels, solve(): pl.pallas_call(functools.partial(solve_kernel, kernel_total, float(pixel_...  5.73 us
    pallas_call x1, Pallas kernels, filter_tables(): pl.pallas_call(functools.partial(tables_kernel, half_width), out_shape=(j...  5.59 us

profile of v1, /device:TPU:125, one launch (start us, length us, event | category | flops | bytes accessed | tf_op | source)
XLA Modules:
  0.0 202.9 jit_solution(1989077917857930821)
XLA Ops:
  0.0 0.1 pad.14.clone
  0.1 0.8 copy.64
  0.9 0.8 copy.65
  1.7 0.1 rev.3
  1.8 0.8 copy.54
  2.6 0.2 convert_reduce_fusion
  2.7 0.6 multiply_add_fusion.1.slot_ref
  3.3 0.2 reduce_window_sum.13
  3.5 0.1 copy.55
  3.6 0.8 fusion
  4.4 0.1 copy.56
  4.5 0.6 reshape.127.send_ref
  5.1 0.1 slice.24
  5.2 0.7 pad_maximum_fusion.y_ref
  5.9 0.6 pad_convert_fusion.x_ref
  6.5 1.5 fusion.6
  8.0 0.3 reduce_sum.48
  8.4 0.3 reduce_sum.49
  8.7 0.1 stack.27
  8.8 0.1 stack.26
  8.9 0.1 copy.62
  9.0 0.6 pad.10.counts
  9.6 107.5 %shard_map.55 = (bf16[4,12,64,384]{3,2,1,0:T(8,128)(2,1)}, f32[4,8,128]{2,1,0:T(8,128)}) custom-call(s32[64]{0:T(128)} %reshape.127.send_ref, s32[32]{0:T(128)} %multiply_add_fusion.1.slot_ref, bf16[16,64,384]{2,1,0:T(8,128)(2,1)} %bitcast.12, f32[4,8,128]{2,1,0:T(8,128)} %pad.10.counts), custom_call_target="tpu_custom_call" | custom-call | tf_op jit(solution)/shard_map/pallas_call | solution.py:137
  117.1 1.0 subtract_reduce_fusion.1
  118.1 0.1 copy.63
  118.2 0.6 convert_element_type.34.bounds_ref
  118.8 5.6 %shard_map.56 = (bf16[2,5120,128]{2,1,0:T(8,128)(2,1)}, bf16[20,2,256,128]{3,2,1,0:T(8,128)(2,1)}) custom-call(f32[40,256]{1,0:T(8,128)} %pad_convert_fusion.x_ref, f32[40,128]{1,0:T(8,128)} %pad_maximum_fusion.y_ref), custom_call_target="tpu_custom_call" | custom-call | tf_op jit(solution)/shard_map/pallas_call | solution.py:190
  124.4 72.8 %shard_map.57.blocks_ref = f32[8,96,128]{2,1,0:T(8,128)} custom-call(s32[16]{0:T(128)} %convert_element_type.34.bounds_ref, bf16[4,12,64,384]{3,2,1,0:T(8,128)(2,1)} %get-tuple-element.10.template_ref.science_ref, bf16[4,12,64,384]{3,2,1,0:T(8,128)(2,1)} %get-tuple-element.10.template_ref.science_ref, bf16[2,5120,128]{2,1,0:T(8,128)(2,1)} %get-tuple-element.11.xtab_ref, ...), custom_call_target="tpu_custom_call" | custom-call | tf_op jit(solution)/shard_map/pallas_call | solution.py:338
  197.2 5.7 %shard_map.58 = f32[8,40]{1,0:T(8,128)} custom-call(f32[8,96,128]{2,1,0:T(8,128)} %shard_map.57.blocks_ref), custom_call_target="tpu_custom_call" | custom-call | tf_op jit(solution)/shard_map/pallas_call | solution.py:399
  (8 shorter events, 0.1 us)
